TPU v7x, 512 devices: a whole 4x4x16 slice. The times are simulated.
512 devices in a mesh: dp: 32 (over z, core), vocab: 16 (over y, x).
Axes of the slice: x: 4, y: 4, z: 16, core: 2. Of those that a mesh axis runs over, the one named last changes fastest.
Arguments:
- hidden: bfloat16 [2, 32, 128, 2048], P(None, 'dp'), may hold values from -320 to 320
- out_weight: bfloat16 [2048, 51200], P('dp', 'vocab'), may hold values from -1 to 1
- targets: int32 [2, 32, 128], P(None, 'dp'), may hold values from 0 to 51199
- prompt_start: int32 [2, 32], P(None, 'dp'), may hold values from 0 to 31
- response_len: int32 [2, 32], P(None, 'dp'), may hold values from 16 to 80, as said below
- partner: int32 [2, 32], P(None, 'dp'), may hold values from 0 to 31, as said below
- ref_scores: float32 [2, 32], P(None, 'dp'), may hold values from -60 to 60
Outputs:
- pair_loss: float32 [2, 32], P(None, 'dp')
- grad_hidden: float32 [2, 32, 128, 2048], P(None, 'dp', None, 'vocab')
Inputs may be any that keep to these rules, and one draw needn't show every extreme that they name: In each microbatch partner pairs the sequences: the partner of the partner of s is s, and it differs from s. `response_len`: the response length of sequence s is below 17 + 64 * (s + 1) // 32.
All inputs are finite; a program needn't handle non-finite values.
Results may differ from a plain program's by a relative error of at most 0.0059.
Values may be sent and summed in bfloat16 or wider, within the bound.
A program may use at most 64 MiB of HBM per device.

v0:
```python
import jax
import jax.numpy as jnp
from jax import lax
from jax.sharding import PartitionSpec as P

margin_beta = 0.1
loss_scale = 65536.0


def from_everyone(value, axis):
    copies = jnp.broadcast_to(value, (lax.axis_size(axis), *value.shape))
    return lax.all_to_all(copies, axis, split_axis=0, concat_axis=0, tiled=True)


def of_everyone(value, axis):
    return from_everyone(value, axis).sum(axis=0)


def all_in_one(value, axis):
    leaves = jax.tree.leaves(value)
    order = sorted(range(len(leaves)), key=lambda k: -leaves[k].size)
    width = (1, *leaves[order[0]].shape)[-1]
    lines = [
        jnp.pad(leaves[k].reshape(-1), (0, -leaves[k].size % width)).reshape(-1, width)
        for k in order
    ]
    both, at, found = (from_everyone(jnp.concatenate(lines), axis), 0, {})
    for k, line in zip(order, lines):
        share = both[:, at : at + len(line)].reshape(len(both), -1)
        found[k] = share[:, : leaves[k].size].reshape(-1, *leaves[k].shape)
        at += len(line)
    numbers = iter(range(len(leaves)))
    return jax.tree.map(lambda _: found[next(numbers)], value)


def joined_by_halves(pieces, combine):
    while len(jax.tree.leaves(pieces)[0]) > 1:
        pieces = jax.vmap(combine)(
            *(jax.tree.map(lambda part: part[side::2], pieces) for side in (0, 1))
        )
    return jax.tree.map(lambda part: part[0], pieces)


def merged(value, axis, combine):
    pieces = all_in_one(value, axis)
    return joined_by_halves(pieces, combine)


def rows_first(arrays, axis, dims):
    turned = [jnp.moveaxis(a, dim, 0) for a, dim in zip(arrays, dims)]
    widths = [t[0].size for t in turned]
    both = jnp.concatenate([t.reshape(-1, w) for t, w in zip(turned, widths)], axis=1)
    out = lax.all_gather(both, axis, axis=0, tiled=True)
    tiles = jnp.split(out, [sum(widths[:k]) for k in range(1, len(widths))], axis=1)
    return tuple(
        (
            jnp.moveaxis(b.reshape(-1, *t.shape[1:]), 0, dim)
            for b, t, dim in zip(tiles, turned, dims)
        )
    )


def in_blocks(value, dim, count):
    dims = value.shape
    tiles = value.reshape(*dims[:dim], count, dims[dim] // count, *dims[dim + 1 :])
    return jnp.moveaxis(tiles, dim, 0)


def summed_on_arrival(value, axis, dim):
    tiles = in_blocks(value, dim, lax.axis_size(axis))
    arrived = lax.all_to_all(tiles, axis, split_axis=0, concat_axis=0, tiled=True)
    return arrived.astype(jnp.float32).sum(axis=0)


def combine_parts(former, latter):
    row_peak = jnp.maximum(former[0], latter[0])
    summed = former[1] * jnp.exp(former[0] - row_peak) + latter[1] * jnp.exp(latter[0] - row_peak)
    return (row_peak, summed, former[2] + latter[2])


def body(hidden, out_weight, targets, prompt_start, response_len, partner, ref_scores):
    micro_count, seq_local, length, model_width = hidden.shape
    lengths_float = response_len.astype(jnp.float32)
    token_total = of_everyone(jnp.sum(lengths_float), "dp")
    full_weight = lax.all_gather(out_weight, "dp", axis=0, tiled=True)
    vocab_cols = full_weight.shape[1]
    row_count = micro_count * seq_local * length
    logits = jnp.dot(
        hidden.reshape(row_count, model_width), full_weight, preferred_element_type=jnp.float32
    )
    vocab_ids = lax.axis_index("vocab") * vocab_cols + lax.broadcasted_iota(
        jnp.int32, (1, vocab_cols), 1
    )
    onehot = targets.reshape(row_count, 1) == vocab_ids
    picked = jnp.sum(jnp.where(onehot, logits, 0.0), axis=1)
    local_peak = jnp.max(logits, axis=1)
    local_sum = jnp.sum(jnp.exp(logits - local_peak[:, None]), axis=1)
    row_peak, summed, target_logit = merged((local_peak, local_sum, picked), "vocab", combine_parts)
    log_total = row_peak + jnp.log(summed)
    token_logp = (target_logit - log_total).reshape(micro_count, seq_local, length)
    position = lax.broadcasted_iota(jnp.int32, (1, 1, length), 2)
    end_pos = prompt_start + response_len
    response_mask = (
        (position >= prompt_start[:, :, None]) & (position < end_pos[:, :, None])
    ).astype(jnp.float32)
    seq_sum = jnp.sum(response_mask * token_logp, axis=2)
    sums_all, refs_all = rows_first((seq_sum, ref_scores), "dp", (1, 1))
    seq_total = sums_all.shape[1]
    mean_length = token_total / (micro_count * seq_total)
    gaps_all = sums_all / mean_length - refs_all
    own_gap = seq_sum / mean_length - ref_scores
    global_ids = lax.broadcasted_iota(jnp.int32, (1, 1, seq_total), 2)
    partner_gap = jnp.sum(
        jnp.where(partner[:, :, None] == global_ids, gaps_all[:, None, :], 0.0), axis=2
    )
    own_index = lax.axis_index("dp") * seq_local + lax.broadcasted_iota(
        jnp.int32, (1, seq_local), 1
    )
    pair_sign = jnp.where(own_index < partner, 1.0, -1.0)
    margin = margin_beta * pair_sign * (own_gap - partner_gap)
    pair_loss = jax.nn.softplus(-margin)
    seq_weight = -loss_scale * margin_beta * pair_sign * jax.nn.sigmoid(-margin) / mean_length
    row_weight = (seq_weight[:, :, None] * response_mask).reshape(row_count, 1)
    softmax = jnp.exp(logits - log_total[:, None])
    grad_logits = (row_weight * (onehot.astype(jnp.float32) - softmax)).astype(jnp.bfloat16)
    partial_grad = lax.dot_general(
        grad_logits, full_weight, (((1,), (1,)), ((), ())), preferred_element_type=jnp.float32
    )
    grad_share = summed_on_arrival(partial_grad.astype(jnp.bfloat16), "vocab", 1)
    return (pair_loss, grad_share.reshape(micro_count, seq_local, length, grad_share.shape[1]))


def solution(mesh):
    return jax.shard_map(
        body,
        mesh=mesh,
        in_specs=(
            P(None, "dp", None, None),
            P("dp", "vocab"),
            P(None, "dp", None),
            P(None, "dp"),
            P(None, "dp"),
            P(None, "dp"),
            P(None, "dp"),
        ),
        out_specs=(P(None, "dp"), P(None, "dp", None, "vocab")),
        check_vma=False,
    )
```

profile of v0, /device:TPU:1, one launch (start us, length us, event | category | flops | bytes accessed | tf_op | source)
XLA Modules:
  0.0 199.4 jit_solution(17480765687842968630)
XLA Ops:
  7.2 0.0 copy-start
  7.2 0.0 all-gather.3.cloned.1.call-start
  7.2 0.7 all-gather.3.cloned.1.call-update
  7.9 1.3 convert_reduce_fusion.1
  9.2 1.3 broadcast_in_dim.33
  10.4 16.7 %all-to-all-start.1 = ((f32[32,1,1]{2,1,0:T(1,128)}), f32[32,1,1]{2,1,0:T(1,128)S(1)}, u32[]{:S(2)}, u32[]{:S(2)}) async-start(f32[32,1,1]{2,1,0:T(1,128)} %broadcast_in_dim.33), calls=%async_computation.1 | async-start | bytes 32768 | tf_op jit(solution)/shard_map/all_to_all | solution.py:12
  27.2 77.1 %all-gather.3.cloned.1.call-done = bf16[2048,3200]{1,0:T(8,128)(2,1)} async-done(((bf16[64,3200]{1,0:T(8,128)(2,1)}), bf16[2048,3200]{1,0:T(8,128)(2,1)}) %all-gather.3.cloned.1.call-update) | async-done | bytes 13107216 | tf_op jit(solution)/shard_map/all_gather | solution.py:85
  104.3 0.0 copy-done
  104.3 0.0 copy-start.4
  104.3 7.4 %fusion.20 = (f32[256]{0:T(256)S(1)}, f32[256,3200]{1,0:T(8,128)S(1)}) fusion(bf16[256,2048]{1,0:T(8,128)(2,1)S(1)} %bitcast.50, bf16[2048,3200]{1,0:T(8,128)(2,1)} %all-gather.3.cloned.1.call-done), kind=kOutput, calls=%fused_computation.48 | convolution fusion | flops 3356262144 | bytes 17433600 | tf_op jit(solution)/shard_map/dot_general | solution.py:88
  111.6 0.0 copy-start.1
  111.6 0.0 copy-start.3
  111.7 0.0 copy-start.6
  111.7 0.0 copy-start.5
  111.7 0.0 copy-start.2
  111.7 1.6 copy-done.1
  113.3 0.0 copy-done.4
  113.3 0.9 exponential_reduce_fusion
  114.2 0.0 all-to-all-done.1
  114.2 0.6 broadcast_in_dim.32
  114.9 6.5 %all-to-all-start = ((f32[16,3,256]{2,1,0:T(4,128)}), f32[16,3,256]{2,1,0:T(4,128)S(1)}, u32[]{:S(2)}, u32[]{:S(2)}) async-start(f32[16,3,256]{2,1,0:T(4,128)} %broadcast_in_dim.32), calls=%async_computation | async-start | bytes 131072 | tf_op jit(solution)/shard_map/all_to_all | solution.py:12
  121.4 0.0 copy-done.3
  121.4 0.0 copy-done.6
  121.4 0.6 reduce_sum.69
  122.7 5.2 %all-to-all-done = f32[16,3,256]{2,1,0:T(4,128)S(1)} async-done(((f32[16,3,256]{2,1,0:T(4,128)}), f32[16,3,256]{2,1,0:T(4,128)S(1)}, u32[]{:S(2)}, u32[]{:S(2)}) %all-to-all-start) | async-done | bytes 49184 | tf_op jit(solution)/shard_map/all_to_all | solution.py:12
  128.4 0.2 fusion.16
  128.6 0.0 copy-done.5
  128.6 0.1 maximum_bitcast_fusion
  128.7 30.1 %all-gather = f32[32,1,4]{2,1,0:T(1,128)S(1)} all-gather(f32[1,1,4]{2,1,0:T(1,128)S(1)} %maximum_bitcast_fusion), channel_id=1, replica_groups=mesh['dp'=32,'vocab'=16] {'dp'}, dimensions={0}, use_global_device_ids=true | all-gather | bytes 528 | tf_op jit(solution)/shard_map/all_gather | solution.py:53
  158.8 0.1 copy.21
  158.9 0.0 copy-done.2
  158.9 0.2 fusion.12
  159.1 0.1 and_select_fusion
  159.2 9.5 %fusion.9 = bf16[32,16,8,128]{3,2,1,0:T(8,128)(2,1)S(1)} fusion(bf16[2048,3200]{1,0:T(8,128)(2,1)} %all-gather.3.cloned.1.call-done, f32[256,3200]{1,0:T(8,128)} %copy-done.1, f32[256]{0:T(256)S(1)} %bitcast.66, f32[256]{0:T(256)S(1)} %bitcast.65, s32[3200]{0:T(1024)S(1)} %iota_add_fusion, s32[256]{0:T(256)S(1)} %bitcast.64), kind=kOutput, calls=%fused_computation.13 | convolution fusion | flops 3360882688 | bytes 17448448 | tf_op jit(solution)/shard_map/dot_general | solution.py:126
  168.7 1.2 copy.32
  170.0 3.7 %all-to-all-start.2 = ((bf16[16,256,128]{2,1,0:T(8,128)(2,1)}), bf16[16,256,128]{2,1,0:T(8,128)(2,1)S(1)}, u32[]{:S(2)}, u32[]{:S(2)}) async-start(bf16[16,256,128]{2,1,0:T(8,128)(2,1)} %bitcast.48), calls=%async_computation.2 | async-start | bytes 2097152 | tf_op jit(solution)/shard_map/all_to_all | solution.py:71
  173.6 0.5 compare_select_fusion.1
  174.1 17.6 %all-to-all-done.2 = bf16[16,256,128]{2,1,0:T(8,128)(2,1)S(1)} async-done(((bf16[16,256,128]{2,1,0:T(8,128)(2,1)}), bf16[16,256,128]{2,1,0:T(8,128)(2,1)S(1)}, u32[]{:S(2)}, u32[]{:S(2)}) %all-to-all-start.2) | async-done | bytes 1048608 | tf_op jit(solution)/shard_map/all_to_all | solution.py:71
  191.8 0.8 convert_reduce_fusion
  (32 shorter events, 0.5 us)
Async XLA Ops:
  7.2 97.1 %copy-start = (bf16[2,1,128,2048]{3,2,1,0:T(8,128)(2,1)S(1)}, bf16[2,1,128,2048]{3,2,1,0:T(8,128)(2,1)}, u32[]{:S(2)}) copy-start(bf16[2,1,128,2048]{3,2,1,0:T(8,128)(2,1)} %param.7) | copy-start | bytes 3145732
  7.2 97.1 %all-gather.3.cloned.1.call-start = ((), (), s32[]{:S(2)}) async-start(), calls=%async_computation.3 | async-start | bytes 13516800 | tf_op jit(solution)/shard_map/all_gather | solution.py:85
  10.4 103.8 %all-to-all-start.1 = ((f32[32,1,1]{2,1,0:T(1,128)}), f32[32,1,1]{2,1,0:T(1,128)S(1)}, u32[]{:S(2)}, u32[]{:S(2)}) async-start(f32[32,1,1]{2,1,0:T(1,128)} %broadcast_in_dim.33), calls=%async_computation.1 | async-start | bytes 32768 | tf_op jit(solution)/shard_map/all_to_all | solution.py:12
  104.3 9.0 %copy-start.4 = (s32[2,1,128]{2,1,0:T(1,128)S(1)}, s32[2,1,128]{2,1,0:T(1,128)}, u32[]{:S(2)}) copy-start(s32[2,1,128]{2,1,0:T(1,128)} %param.9) | copy-start | bytes 3076
  111.6 1.7 copy-start.1
  111.6 9.8 %copy-start.3 = (s32[2,1]{0,1:T(1,128)S(1)}, s32[2,1]{0,1:T(1,128)}, u32[]{:S(2)}) copy-start(s32[2,1]{0,1:T(1,128)} %param.10) | copy-start | bytes 28
  111.7 9.8 %copy-start.6 = (s32[2,1]{0,1:T(1,128)S(1)}, s32[2,1]{0,1:T(1,128)}, u32[]{:S(2)}) copy-start(s32[2,1]{0,1:T(1,128)} %param.11) | copy-start | bytes 28
  111.7 17.0 %copy-start.5 = (f32[2,1]{0,1:T(1,128)S(1)}, f32[2,1]{0,1:T(1,128)}, u32[]{:S(2)}) copy-start(f32[2,1]{0,1:T(1,128)} %param.13) | copy-start | bytes 28
  111.7 47.2 %copy-start.2 = (s32[2,1]{0,1:T(1,128)S(1)}, s32[2,1]{0,1:T(1,128)}, u32[]{:S(2)}) copy-start(s32[2,1]{0,1:T(1,128)} %param.12) | copy-start | bytes 28
  114.9 13.1 %all-to-all-start = ((f32[16,3,256]{2,1,0:T(4,128)}), f32[16,3,256]{2,1,0:T(4,128)S(1)}, u32[]{:S(2)}, u32[]{:S(2)}) async-start(f32[16,3,256]{2,1,0:T(4,128)} %broadcast_in_dim.32), calls=%async_computation | async-start | bytes 131072 | tf_op jit(solution)/shard_map/all_to_all | solution.py:12
  170.0 21.8 %all-to-all-start.2 = ((bf16[16,256,128]{2,1,0:T(8,128)(2,1)}), bf16[16,256,128]{2,1,0:T(8,128)(2,1)S(1)}, u32[]{:S(2)}, u32[]{:S(2)}) async-start(bf16[16,256,128]{2,1,0:T(8,128)(2,1)} %bitcast.48), calls=%async_computation.2 | async-start | bytes 2097152 | tf_op jit(solution)/shard_map/all_to_all | solution.py:71
Sparse Core Ops, SparseCore 0:
  10.1 94.1 all-gather.2
where the time goes:
time: 200 us; the launch traced here: 199 us
  waiting for transfers between devices  101 us (50%)
  blocking collectives  30.1 us (15%)
  starting transfers between devices  27 us (14%)
  matrix products  16.9 us (8%)
  between operations  14.9 us (7%)
  local copies, waits for them, and re-layouts  5.29 us (3%)
  other arithmetic  4.75 us (2%)
    all_gather x1, waiting for transfers between devices, body(): full_weight = lax.all_gather(out_weight, 'dp', axis=0, tiled=True)  77.1 us
    all_gather x1, blocking collectives, rows_first(): out = lax.all_gather(both, axis, axis=0, tiled=True)  30.1 us
    all_to_all x2, starting transfers between devices, from_everyone(): return lax.all_to_all(copies, axis, split_axis=0, concat_axis=0, tiled=True)  23.3 us
    all_to_all x1, waiting for transfers between devices, summed_on_arrival(): lax.all_to_all(tiles, axis, split_axis=0, concat_axis=0, tiled=True)  17.6 us
    dot_general x1, matrix products, body(): lax.dot_general(grad_logits, full_weight, (((1,), (1,)), ((), ())), prefe...  9.5 us
    dot_general x1, matrix products, body(): jnp.dot(hidden.reshape(row_count, model_width), full_weight, preferred_el...  7.36 us
    all_to_all x2, waiting for transfers between devices, from_everyone(): return lax.all_to_all(copies, axis, split_axis=0, concat_axis=0, tiled=True)  5.2 us
  transfers between devices with their start and end apart: 4, of which 3 were waited for; matrix products, arithmetic and copies ran while one was open for 6% of the time, Pallas kernels for 0%

commit v1 on v0

v1 whole, which is shorter than its diff:
```python
import functools

import jax
import jax.numpy as jnp
from jax import lax
from jax.experimental import pallas as pl
from jax.experimental.pallas import tpu as pltpu
from jax.sharding import PartitionSpec as P

MESH = pl.DeviceIdType.MESH
margin_beta = 0.1
loss_scale = 65536.0
window = 80
chunk_rows = 16


def kernel(
    dp_n, nv, h_ref, w_hbm, t_ref, start_ref, len_ref, partner_ref, refs_ref,
    loss_ref, grad_ref,
    wg, hc, logits, gl, stat, gsend, grecv, msg,
    own_sem, ring_s, ring_r, sib_s, sib_r, stat_s, stat_r, msg_s, msg_r, g_s, g_r,
):
    dp, v = lax.axis_index("dp"), lax.axis_index("vocab")
    nz, steps = dp_n // 2, dp_n // 4
    z = dp // 2
    sib_id = dp + 1 - 2 * lax.rem(dp, 2)
    kr, cols = w_hbm.shape
    depth = hc.shape[1]
    dcol = depth // nv
    nc = kr // chunk_rows
    ck = 2 * kr
    rows_n = 2 * window
    ncol = cols // 5
    f32, bf16 = jnp.float32, jnp.bfloat16

    def rows(owner, j):
        return pl.ds(pl.multiple_of(owner * kr + j * chunk_rows, chunk_rows), chunk_rows)

    own_rows = pl.ds(pl.multiple_of(dp * kr, kr), kr)
    own_copy = pltpu.make_async_copy(w_hbm, wg.at[own_rows], own_sem)
    own_copy.start()

    bar = pltpu.get_barrier_semaphore()

    @pl.loop(1, dp_n)
    def _(k):
        pl.semaphore_signal(bar, inc=1, device_id=(lax.rem(dp + k, dp_n), v), device_id_type=MESH)

    @pl.loop(1, nv)
    def _(k):
        pl.semaphore_signal(bar, inc=1, device_id=(dp, lax.rem(v + k, nv)), device_id_type=MESH)

    own_copy.wait()
    pl.semaphore_wait(bar, dp_n - 1 + nv - 1)

    def owner_of(d, h):
        back = (dp_n - 2) * h if d == 0 else 2 * h
        return lax.rem(dp + back, dp_n)

    def ring(d, h, j, owner):
        to = lax.rem(dp + (2 if d == 0 else dp_n - 2), dp_n)
        return pltpu.make_async_remote_copy(
            src_ref=wg.at[rows(owner, j)], dst_ref=wg.at[rows(owner, j)],
            send_sem=ring_s.at[d, h, j], recv_sem=ring_r.at[d, h, j],
            device_id=(to, v), device_id_type=MESH,
        )

    def send(d, h, j):
        return ring(d, h, j, owner_of(d, h))

    def arrived(d, h, j):
        ring(d, h, j, owner_of(d, h + 1)).wait_recv()

    def sib(d, h, j, owner):
        return pltpu.make_async_remote_copy(
            src_ref=wg.at[rows(owner, j)], dst_ref=wg.at[rows(owner, j)],
            send_sem=sib_s.at[d, h, j], recv_sem=sib_r.at[d, h, j],
            device_id=(sib_id, v), device_id_type=MESH,
        )

    def twin(owner):
        return owner + 1 - 2 * lax.rem(owner, 2)

    for j in range(nc):
        for d in (0, 1):
            send(d, 0, j).start()
    for j in range(nc):
        sib(0, steps, j, dp).start()

    starts = [start_ref[m : m + 1, 0:1] for m in (0, 1)]
    lens = [len_ref[m : m + 1, 0:1] for m in (0, 1)]
    tcols, masks = [], []
    for m in (0, 1):
        pos = lax.broadcasted_iota(jnp.int32, (window, 128), 1)
        row = lax.broadcasted_iota(jnp.int32, (window, 128), 0)
        pick = pos == row + starts[m]
        pick_f = pick.astype(f32)
        tcols.append(jnp.sum(pick_f * t_ref[m : m + 1, :].astype(f32), axis=1, keepdims=True))
        rowc = lax.broadcasted_iota(jnp.int32, (window, 1), 0)
        masks.append((rowc < lens[m]).astype(f32))
        sel = pick_f.astype(bf16)

        @pl.loop(0, depth // 512)
        def _(c):
            at = pl.ds(pl.multiple_of(c * 512, 512), 512)
            got = jnp.dot(sel, h_ref[m * 128 : m * 128 + 128, at], preferred_element_type=f32)
            hc[m * window : (m + 1) * window, at] = got.astype(bf16)

    local_t = jnp.concatenate(tcols, axis=0) - (v * cols).astype(f32)

    def chip_rows(zz):
        return pl.ds(pl.multiple_of(zz * ck, ck), ck)

    def accumulate(zs, first):
        hs = [hc[:, chip_rows(zz)] for zz in zs]
        lhs = hs[0] if len(hs) == 1 else jnp.concatenate(hs, axis=1)

        @pl.loop(0, cols // ncol)
        def _(c):
            at = pl.ds(pl.multiple_of(c * ncol, 128), ncol)
            ws = [wg[chip_rows(zz), at] for zz in zs]
            rhs = ws[0] if len(ws) == 1 else jnp.concatenate(ws, axis=0)
            got = jnp.dot(lhs, rhs, preferred_element_type=f32)
            if first:
                logits[:, at] = got
            else:
                logits[:, at] += got

    half = nc // 2
    full_js = (tuple(range(nc)), tuple(range(nc)))
    half_js = (tuple(range(half)), tuple(range(half, nc)))

    def relay(h, js, forward):
        for j in range(nc):
            for d in (0, 1):
                if j in js[d]:
                    arrived(d, h, j)
                    if j in forward[d]:
                        send(d, h + 1, j).start()
                    sib(d, h, j, owner_of(d, h + 1)).start()

    def compute(h):
        for j in range(nc):
            for d in (0, 1):
                sib(d, h, j, twin(owner_of(d, h + 1))).wait_recv()
        accumulate((lax.rem(z + nz - h - 1, nz), lax.rem(z + h + 1, nz)), False)

    for j in range(nc):
        sib(0, steps, j, sib_id).wait_recv()
    accumulate((z,), True)

    none = ((), ())

    @pl.loop(0, steps - 2)
    def _(h):
        relay(h, full_js, full_js)

        @pl.when(h > 0)
        def _():
            compute(h - 1)

    if steps > 2:
        relay(steps - 2, full_js, half_js)
        compute(steps - 3)
    else:
        relay(0, full_js, half_js)
    relay(steps - 1, half_js, none)
    compute(steps - 2)
    for d in (0, 1):
        for j in half_js[d]:
            sib(d, steps - 1, j, twin(owner_of(d, steps))).wait_recv()
    accumulate((lax.rem(z + steps, nz),), False)

    nt = cols // ncol

    def ids(c):
        at = lax.broadcasted_iota(jnp.int32, (1, ncol), 1) + c * ncol
        return at.astype(f32)

    def cut(c):
        return pl.ds(pl.multiple_of(c * ncol, 128), ncol)

    peak = lax.fori_loop(
        0, nt,
        lambda c, m: jnp.maximum(m, jnp.max(logits[:, cut(c)], axis=1, keepdims=True)),
        jnp.full((rows_n, 1), -jnp.inf, f32),
    )

    def tally(c, carry):
        total, target = carry
        part = logits[:, cut(c)]
        total = total + jnp.sum(jnp.exp(part - peak), axis=1, keepdims=True)
        target = target + jnp.sum(jnp.where(local_t == ids(c), part, 0.0), axis=1, keepdims=True)
        return total, target

    zero = jnp.zeros((rows_n, 1), f32)
    total, target = lax.fori_loop(0, nt, tally, (zero, zero))
    lane = lax.broadcasted_iota(jnp.int32, (rows_n, 128), 1)
    table = jnp.where(lane == 0, peak, jnp.where(lane == 1, total, jnp.where(lane == 2, target, 0.0)))
    table = jnp.concatenate([table, jnp.zeros((256 - rows_n, 128), f32)], axis=0)
    stat[v] = jnp.transpose(table)[0:8, :]

    def stat_copy(peer, slot):
        return pltpu.make_async_remote_copy(
            src_ref=stat.at[slot], dst_ref=stat.at[slot],
            send_sem=stat_s.at[peer], recv_sem=stat_r.at[slot],
            device_id=(dp, peer), device_id_type=MESH,
        )

    @pl.loop(1, nv)
    def _(k):
        stat_copy(lax.rem(v + k, nv), v).start()

    @pl.loop(1, nv)
    def _(k):
        peer = lax.rem(v + k, nv)
        stat_copy(peer, peer).wait_recv()

    top = stat[0, 0:1, :]
    for k in range(1, nv):
        top = jnp.maximum(top, stat[k, 0:1, :])
    whole = jnp.zeros_like(top)
    hit = jnp.zeros_like(top)
    for k in range(nv):
        whole = whole + stat[k, 1:2, :] * jnp.exp(stat[k, 0:1, :] - top)
        hit = hit + stat[k, 2:3, :]
    log_total = top + jnp.log(whole)
    token = hit - log_total
    spot = lax.broadcasted_iota(jnp.int32, (1, 256), 1)
    sums = []
    for m in (0, 1):
        inside = (spot >= m * window) & (spot < m * window + lens[m])
        sums.append(jnp.sum(jnp.where(inside, token, 0.0), axis=1, keepdims=True))

    refs = [refs_ref[m : m + 1, 0:1] for m in (0, 1)]
    count = (lens[0] + lens[1]).astype(f32)
    ml = lax.broadcasted_iota(jnp.int32, (8, 128), 1)
    mr = lax.broadcasted_iota(jnp.int32, (8, 128), 0)
    word = jnp.zeros((8, 128), f32)
    for at, value in enumerate((sums[0], sums[1], refs[0], refs[1], count)):
        word = jnp.where((ml == at) & (mr == 0), value, word)
    msg[dp] = word

    def msg_copy(peer, slot):
        return pltpu.make_async_remote_copy(
            src_ref=msg.at[slot], dst_ref=msg.at[slot],
            send_sem=msg_s.at[peer], recv_sem=msg_r.at[slot],
            device_id=(peer, v), device_id_type=MESH,
        )

    @pl.loop(1, dp_n)
    def _(k):
        msg_copy(lax.rem(dp + k, dp_n), dp).start()

    lt_col = jnp.transpose(jnp.broadcast_to(log_total, (128, 256)))[0:rows_n, 0:1]

    @pl.loop(0, nt)
    def _(c):
        soft = jnp.exp(logits[:, cut(c)] - lt_col)
        onehot = (local_t == ids(c)).astype(f32)
        gl[:, cut(c)] = (onehot - soft).astype(bf16)

    def g_copy(peer, slot):
        return pltpu.make_async_remote_copy(
            src_ref=gsend.at[peer], dst_ref=grecv.at[slot],
            send_sem=g_s.at[peer], recv_sem=g_r.at[slot],
            device_id=(dp, peer), device_id_type=MESH,
        )

    npair = nv // 2

    @pl.loop(0, npair)
    def _(i):
        q = lax.rem(v // 2 + i + 1, npair)
        at = pl.ds(pl.multiple_of(q * 2 * dcol, 128), 2 * dcol)
        got = lax.dot_general(
            gl[...], wg[at, :], (((1,), (1,)), ((), ())), preferred_element_type=f32
        ).astype(bf16)
        for side in (0, 1):
            peer = 2 * q + side
            gsend[peer] = got[:, side * dcol : (side + 1) * dcol]

            @pl.when(peer != v)
            def _():
                g_copy(peer, v).start()

    @pl.loop(1, dp_n)
    def _(k):
        peer = lax.rem(dp + k, dp_n)
        msg_copy(peer, peer).wait_recv()

    board = jnp.sum(msg[...], axis=1)
    mean_length = jnp.sum(board[:, 4:5], axis=0, keepdims=True) / float(2 * dp_n)
    who = lax.broadcasted_iota(jnp.int32, (dp_n, 1), 0)
    weights = []
    loss_lane = lax.broadcasted_iota(jnp.int32, (8, 128), 0)
    losses = jnp.zeros((8, 128), f32)
    for m in (0, 1):
        gaps = board[:, m : m + 1] / mean_length - board[:, 2 + m : 3 + m]
        own_gap = sums[m] / mean_length - refs[m]
        partner = partner_ref[m : m + 1, 0:1]
        partner_gap = jnp.sum(jnp.where(who == partner, gaps, 0.0), axis=0, keepdims=True)
        sign = jnp.where(dp < partner, 1.0, -1.0)
        margin = margin_beta * sign * (own_gap - partner_gap)
        small = jnp.exp(-jnp.abs(margin))
        loss = jnp.maximum(-margin, 0.0) + jnp.log1p(small)
        sig = jnp.where(margin >= 0, small, 1.0) / (1.0 + small)
        weights.append(-loss_scale * margin_beta * sign * sig / mean_length)
        losses = jnp.where(loss_lane == m, loss, losses)
    loss_ref[...] = losses

    @pl.loop(1, nv)
    def _(k):
        peer = lax.rem(v + k, nv)
        g_copy(peer, peer).wait_recv()

    summed = lax.fori_loop(
        1, nv,
        lambda k, acc: acc + grecv[lax.rem(v + k, nv)].astype(f32),
        gsend[v].astype(f32),
    )
    for m in (0, 1):
        part = summed[m * window : (m + 1) * window] * (masks[m] * weights[m])
        pos = lax.broadcasted_iota(jnp.int32, (128, window), 0)
        row = lax.broadcasted_iota(jnp.int32, (128, window), 1)
        back = (pos == row + starts[m]).astype(f32)
        grad_ref[m] = jnp.dot(
            back, part, preferred_element_type=f32, precision=lax.Precision.HIGHEST
        )

    @pl.loop(1, nv)
    def _(k):
        peer = lax.rem(v + k, nv)
        stat_copy(peer, v).wait_send()
        g_copy(peer, v).wait_send()

    @pl.loop(1, dp_n)
    def _(k):
        msg_copy(lax.rem(dp + k, dp_n), dp).wait_send()

    @pl.loop(0, steps - 1)
    def _(h):
        for j in range(nc):
            for d in (0, 1):
                send(d, h, j).wait_send()
                sib(d, h, j, owner_of(d, h + 1)).wait_send()

    for d in (0, 1):
        for j in half_js[d]:
            send(d, steps - 1, j).wait_send()
            sib(d, steps - 1, j, owner_of(d, steps)).wait_send()
    for j in range(nc):
        sib(0, steps, j, dp).wait_send()


def solution(mesh):
    dp_n, nv = mesh.shape["dp"], mesh.shape["vocab"]
    steps = dp_n // 4

    def body(hidden, out_weight, targets, prompt_start, response_len, partner, ref_scores):
        micro, seqs, length, depth = hidden.shape
        kr, cols = out_weight.shape
        nc = kr // chunk_rows
        rows_n = 2 * window
        dcol = depth // nv
        f32, bf16 = jnp.float32, jnp.bfloat16
        vm = pl.BlockSpec(memory_space=pltpu.VMEM)
        dma = pltpu.SemaphoreType.DMA
        loss, grad = pl.pallas_call(
            functools.partial(kernel, dp_n, nv),
            out_shape=(
                jax.ShapeDtypeStruct((8, 128), f32),
                jax.ShapeDtypeStruct((micro, length, dcol), f32),
            ),
            in_specs=[vm, pl.BlockSpec(memory_space=pl.ANY), vm, vm, vm, vm, vm],
            out_specs=(vm, vm),
            scratch_shapes=[
                pltpu.VMEM((depth, cols), bf16),
                pltpu.VMEM((rows_n, depth), bf16),
                pltpu.VMEM((rows_n, cols), f32),
                pltpu.VMEM((rows_n, cols), bf16),
                pltpu.VMEM((nv, 8, 256), f32),
                pltpu.VMEM((nv, rows_n, dcol), bf16),
                pltpu.VMEM((nv, rows_n, dcol), bf16),
                pltpu.VMEM((dp_n, 8, 128), f32),
                dma,
                dma((2, steps, nc)),
                dma((2, steps, nc)),
                dma((2, steps + 1, nc)),
                dma((2, steps + 1, nc)),
                dma((nv,)), dma((nv,)),
                dma((dp_n,)), dma((dp_n,)),
                dma((nv,)), dma((nv,)),
            ],
            compiler_params=pltpu.CompilerParams(
                collective_id=0, has_side_effects=True, vmem_limit_bytes=48 * 1024 * 1024
            ),
        )(
            hidden.reshape(micro * length, depth),
            out_weight,
            targets.reshape(micro, length),
            prompt_start,
            response_len,
            partner,
            ref_scores,
        )
        return loss[0:2, 0:1], grad.reshape(micro, seqs, length, dcol)

    return jax.shard_map(
        body,
        mesh=mesh,
        in_specs=(
            P(None, "dp", None, None),
            P("dp", "vocab"),
            P(None, "dp", None),
            P(None, "dp"),
            P(None, "dp"),
            P(None, "dp"),
            P(None, "dp"),
        ),
        out_specs=(P(None, "dp"), P(None, "dp", None, "vocab")),
        check_vma=False,
    )
```

time: 200 us -> 120 us (0.60)
  Pallas kernels: 0 us -> 112 us
  waiting for transfers between devices: 101 us -> 0 us
  blocking collectives: 30.1 us -> 0 us
  starting transfers between devices: 27 us -> 0 us
  matrix products: 16.9 us -> 0 us
  between operations: 14.9 us -> 0.66 us
  other arithmetic: 4.75 us -> 0 us
    pallas_call x0 -> x1, Pallas kernels: none -> 112 us  [body(): pl.pallas_call(functools.partial(kernel, dp_n, nv), out_shape=(jax.ShapeD...]
    all_gather x1 -> x0, waiting for transfers between devices: 77.1 us -> none  [body(): full_weight = lax.all_gather(out_weight, 'dp', axis=0, tiled=True)]
    all_gather x1 -> x0, blocking collectives: 30.1 us -> none  [rows_first(): out = lax.all_gather(both, axis, axis=0, tiled=True)]
    all_to_all x3 -> x0, starting transfers between devices: 26.9 us -> none  [the longest x2 23.3 us: from_everyone(): return lax.all_to_all(copies, axis, split_axis=0, concat_axis=0, tiled=True)]
    all_to_all x3 -> x0, waiting for transfers between devices: 22.8 us -> none  [the longest x1 17.6 us: summed_on_arrival(): lax.all_to_all(tiles, axis, split_axis=0, concat_axis=0, tiled=True)]
    dot_general x2 -> x0, matrix products: 16.9 us -> none  [the longest x1 9.5 us: body(): lax.dot_general(grad_logits, full_weight, (((1,), (1,)), ((), ())), prefe...]
    unnamed x15 -> x20, local copies, waits for them, and re-layouts: 1.66 us -> 6.77 us
    reduce_sum x6 -> x0, other arithmetic: 3.95 us -> none  [the longest x1 1.26 us: body(): token_total = of_everyone(jnp.sum(lengths_float), 'dp')]
  transfers between devices with their start and end apart: 4 -> 0, of which waited for: 3 -> 0; matrix products, arithmetic and copies ran while one was open for 6% -> 0% of each run, Pallas kernels for 0% -> 0%
where the time goes in v1:
time: 120 us
  Pallas kernels  112 us (93%)
  local copies, waits for them, and re-layouts  6.77 us (6%)
    pallas_call x1, Pallas kernels, body(): pl.pallas_call(functools.partial(kernel, dp_n, nv), out_shape=(jax.ShapeD...  112 us
    unnamed x20, local copies, waits for them, and re-layouts  6.77 us

profile of v1, /device:TPU:1, one launch (start us, length us, event | category | flops | bytes accessed | tf_op | source)
XLA Modules:
  0.0 119.8 jit_solution(8665037476947014503)
XLA Ops:
  0.6 0.0 copy-start.3
  0.6 0.6 copy-done.3
  1.3 0.0 copy-start.4
  1.3 0.1 copy.9.start_ref
  1.4 0.6 copy-done.4
  1.9 0.0 copy-start.5
  1.9 0.1 copy.10.len_ref
  2.0 0.6 copy-done.5
  2.6 0.0 copy-start.6
  2.6 0.1 copy.11.partner_ref
  2.7 0.6 copy-done.6
  3.3 0.0 copy-start.2
  3.3 0.1 copy.12.refs_ref
  3.3 0.6 copy-done.2
  3.9 0.0 copy-start
  3.9 1.2 %copy-done = bf16[2,1,128,2048]{3,2,1,0:T(8,128)(2,1)S(1)} copy-done((bf16[2,1,128,2048]{3,2,1,0:T(8,128)(2,1)S(1)}, bf16[2,1,128,2048]{3,2,1,0:T(8,128)(2,1)}, u32[]{:S(2)}) %copy-start) | copy-done | bytes 1048600
  5.2 0.0 copy-start.1
  5.2 1.0 copy-done.1
  6.2 112.4 %shard_map.86 = (f32[8,128]{1,0:T(8,128)S(1)}, f32[2,128,128]{2,1,0:T(8,128)S(1)}) custom-call(bf16[256,2048]{1,0:T(8,128)(2,1)S(1)} %bitcast.5, bf16[64,3200]{1,0:T(8,128)(2,1)S(1)} %copy-done.1, s32[2,128]{1,0:T(2,128)S(1)} %bitcast.7, s32[2,1]{1,0:T(2,128)S(1)} %copy.9.start_ref, s32[2,1]{1,0:T(2,128)S(1)} %copy.10.len_ref, s32[2,1]{1,0:T(2,128)S(1)} %copy.11.partner_ref, ...), custom_call_target="tpu_custom_call" | custom-call | tf_op jit(solution)/shard_map/pallas_call | solution.py:369
  118.5 0.6 copy.13
  119.1 0.7 copy.16
  (1 shorter events, 0.0 us)
Async XLA Ops:
  0.6 0.7 copy-start.3
  1.3 0.7 copy-start.4
  1.9 0.7 copy-start.5
  2.6 0.7 copy-start.6
  3.3 0.7 copy-start.2
  3.9 1.2 %copy-start = (bf16[2,1,128,2048]{3,2,1,0:T(8,128)(2,1)S(1)}, bf16[2,1,128,2048]{3,2,1,0:T(8,128)(2,1)}, u32[]{:S(2)}) copy-start(bf16[2,1,128,2048]{3,2,1,0:T(8,128)(2,1)} %param.7) | copy-start | bytes 3145732
  5.2 1.0 copy-start.1

commit v2 on v1

v2 whole, which is shorter than its diff:
```python
import functools

import jax
import jax.numpy as jnp
from jax import lax
from jax.experimental import pallas as pl
from jax.experimental.pallas import tpu as pltpu
from jax.sharding import PartitionSpec as P

MESH = pl.DeviceIdType.MESH
margin_beta = 0.1
loss_scale = 65536.0
window = 80
groups = 2
spread_at = 2
begin_at = 4


def kernel(
    dp_n, nv, h_hbm, w_hbm, t_hbm, start_hbm, len_hbm, partner_hbm, refs_hbm,
    loss_ref, grad_ref,
    h_ref, t_ref, start_ref, len_ref, partner_ref, refs_ref,
    wt, hall, hx, tg, logits, gl, stat, zstat, gsend, grecv, fsend, frecv, msg,
    in_sem, own_sem, ring_s, ring_r, sib_s, sib_r, hx_s, hx_r, tg_s, tg_r, hb_s, hb_r,
    zst_s, zst_r, stat_s, stat_r, msg_s, msg_r, g_s, g_r, f_s, f_r,
):
    f32, bf16 = jnp.float32, jnp.bfloat16
    dp, v = lax.axis_index("dp"), lax.axis_index("vocab")
    nz = dp_n // 2
    z, core = lax.div(dp, 2), lax.rem(dp, 2)
    sib_id = dp + 1 - 2 * core
    kr, cols = w_hbm.shape
    depth = hall.shape[2]
    dcol = depth // nv
    nt = cols // 128
    arc = nz // groups
    far = (nz - arc) // 2
    seg = 2 * window
    rows_n = groups * seg
    ck = 2 * kr
    lanes = zstat.shape[2]
    kz, zlow = lax.div(z, arc), lax.rem(z, arc)

    inputs = [
        pltpu.make_async_copy(src, dst, in_sem.at[k])
        for k, (src, dst) in enumerate((
            (h_hbm, h_ref), (t_hbm, t_ref), (start_hbm, start_ref), (len_hbm, len_ref),
            (partner_hbm, partner_ref), (refs_hbm, refs_ref),
        ))
    ]
    for copy in inputs:
        copy.start()

    def first_tile(p):
        return lax.div(nt * p + nz - 1, nz)

    base = z + 2 * nz - arc + 1
    tile_base = first_tile(base)
    tile_lo = lax.rem(tile_base, nt)
    n_mine = first_tile(base + arc) - tile_base

    def rows_of(owner):
        return pl.ds(pl.multiple_of(owner * kr, kr), kr)

    def own_copy(t):
        at = pl.ds(pl.multiple_of(t * 128, 128), 128)
        slot = lax.rem(t + nt - tile_lo, nt)
        return pltpu.make_async_copy(w_hbm.at[:, at], wt.at[slot, rows_of(dp)], own_sem.at[t])

    @pl.loop(0, nt)
    def _(t):
        own_copy(t).start()

    bar = pltpu.get_barrier_semaphore()

    @pl.loop(1, dp_n)
    def _(k):
        pl.semaphore_signal(bar, inc=1, device_id=(lax.rem(dp + k, dp_n), v), device_id_type=MESH)

    @pl.loop(1, nv)
    def _(k):
        pl.semaphore_signal(bar, inc=1, device_id=(dp, lax.rem(v + k, nv)), device_id_type=MESH)

    for copy in inputs:
        copy.wait()

    def seg_rows(k):
        return pl.ds(pl.multiple_of(k * seg, 16), seg)

    starts = [start_ref[0:1, m : m + 1] for m in (0, 1)]
    lens = [len_ref[0:1, m : m + 1] for m in (0, 1)]
    tcols, masks = [], []
    for m in (0, 1):
        pos = lax.broadcasted_iota(jnp.int32, (window, 128), 1)
        row = lax.broadcasted_iota(jnp.int32, (window, 128), 0)
        pick_f = (pos == row + starts[m]).astype(f32)
        tcols.append(jnp.sum(pick_f * t_ref[m : m + 1, :].astype(f32), axis=1, keepdims=True))
        masks.append(lax.broadcasted_iota(jnp.int32, (window, 1), 0) < lens[m])
        sel = pick_f.astype(bf16)

        @pl.loop(0, depth // 512)
        def _(c):
            at = pl.ds(pl.multiple_of(c * 512, 512), 512)
            got = jnp.dot(sel, h_ref[m * 128 : m * 128 + 128, at], preferred_element_type=f32)
            hall[2 * kz + m, :, at] = got.astype(bf16)

    tcol = jnp.concatenate(tcols + [jnp.zeros((256 - seg, 1), f32)], axis=0)
    tg[kz] = jnp.transpose(jnp.broadcast_to(tcol, (256, 128)))[0:8, :]

    @pl.loop(0, nt)
    def _(t):
        own_copy(t).wait()

    pl.semaphore_wait(bar, dp_n - 1 + nv - 1)

    def tall(k):
        s = 2 * (zlow + k * arc) + core
        return lax.div(31 + lax.div(64 * (s + 1), dp_n), 16)

    def by_rows(k, act):
        for size in (2, 3, 4, 5):
            pl.when(tall(k) == size)(functools.partial(act, 16 * size))

    def plane_dev(k):
        return 2 * (zlow + k * arc) + core

    mine = pl.ds(pl.multiple_of(v * dcol, 128), dcol)

    def both(k, size):
        return pl.ds(2 * k, 2), pl.ds(0, size)

    def hx_copy(slot, size, to):
        return pltpu.make_async_remote_copy(
            src_ref=hall.at[(*both(slot, size), mine)], dst_ref=hx.at[both(slot, size)],
            send_sem=hx_s.at[to], recv_sem=hx_r.at[slot],
            device_id=(plane_dev(to), v), device_id_type=MESH,
        )

    def tg_copy(slot, to):
        return pltpu.make_async_remote_copy(
            src_ref=tg.at[slot], dst_ref=tg.at[slot],
            send_sem=tg_s.at[to], recv_sem=tg_r.at[slot],
            device_id=(plane_dev(to), v), device_id_type=MESH,
        )

    others = [lax.rem(kz + k, groups) for k in range(1, groups)]
    for to in others:
        by_rows(kz, lambda size: hx_copy(kz, size, to).start())
        tg_copy(kz, to).start()

    sizes = range(nt // nz, -(-nt // nz) + 1)

    def by_tiles(x, act):
        t0 = first_tile(x)
        n = first_tile(x + 1) - t0
        for size in sizes:
            pl.when(n == size)(functools.partial(act, t0 - tile_base, size))

    def ring(d, p, e, src, dst, size, owner, step):
        to = lax.rem(dp + 2 * step, dp_n)
        at = rows_of(owner)
        return pltpu.make_async_remote_copy(
            src_ref=wt.at[pl.ds(src, size), at], dst_ref=wt.at[pl.ds(dst, size), at],
            send_sem=ring_s.at[d, p, e], recv_sem=ring_r.at[d, p, e],
            device_id=(to, v), device_id_type=MESH,
        )

    ahead = (first_tile(base + 1) - tile_base, first_tile(base - 1) - tile_base)

    def place(d, p):
        return base + arc - 1 - p if d == 0 else base + p

    def owner_at(d, e):
        return 2 * lax.rem(z + (nz - e if d == 0 else e), nz) + core

    def direct(d, e, act):
        if d == 0:
            shift = first_tile(base + e) - tile_base
            by_tiles(base + e + arc - 1, lambda src, size: act(
                ring(0, 0, e, src, src - shift, size, dp, e)))
        else:
            by_tiles(base + nz - e, lambda src, size: act(
                ring(1, 0, e, src, 0, size, dp, nz - e)))

    def onward(d, p, e, act):
        owner = owner_at(d, e - 1)
        by_tiles(place(d, p), lambda src, size: act(
            ring(d, p + 1, e, src, src - ahead[d], size, owner, 1 if d == 0 else nz - 1)))

    def sib(rel, x, src, size, who):
        at = rows_of(2 * lax.rem(z + rel, nz) + who)
        return pltpu.make_async_remote_copy(
            src_ref=wt.at[pl.ds(src, size), at], dst_ref=wt.at[pl.ds(src, size), at],
            send_sem=sib_s.at[rel, x], recv_sem=sib_r.at[rel, x],
            device_id=(sib_id, v), device_id_type=MESH,
        )

    start = lambda copy: copy.start()
    sent = lambda copy: copy.wait_send()

    @pl.loop(1, far + 1)
    def _(k):
        for d in (0, 1):
            direct(d, far + 1 - k, start)

    @pl.loop(0, arc - 1)
    def _(p):
        for d in (0, 1):
            onward(d, p, 1, start)

    @pl.loop(0, arc)
    def _(x):
        by_tiles(base + x, lambda src, size: sib(0, x, src, size, core).start())

    def take(d, p, e):
        owner = owner_at(d, e)
        rel = nz - e if d == 0 else e
        x = arc - 1 - p if d == 0 else p

        def act(src, size):
            ring(d, p, e, src, src, size, owner, 1).wait_recv()

            @pl.when(p < arc - 1)
            def _():
                ring(d, p + 1, e + 1, src, src - ahead[d], size, owner, 1 if d == 0 else nz - 1).start()

            sib(rel, x, src, size, core).start()

        by_tiles(place(d, p), act)

    def relay(s):
        @pl.loop(0, far)
        def _(k):
            for d in (0, 1):
                take(d, s - 1, far + s - 1 - k)

        @pl.loop(s, arc)
        def _(p):
            for d in (0, 1):
                take(d, p, s)

    pairs = gl.shape[1] // 256

    def tile(i):
        return jnp.minimum(i, n_mine - 1)

    def shard_tile(i):
        return lax.rem(tile_lo + tile(i), nt)

    def chip_rows(rel):
        return pl.ds(pl.multiple_of(lax.rem(z + rel, nz) * ck, ck), ck)

    def ready(rel, low, high):
        @pl.loop(low, high)
        def _(x):
            by_tiles(base + x, lambda src, size: sib(rel, x, src, size, 1 - core).wait_recv())

    def accumulate(rels, first, low=0, high=pairs):
        lhs = jnp.concatenate(
            [hall[:, :, chip_rows(rel)].reshape(rows_n, ck) for rel in rels], axis=1
        )

        @pl.loop(low, high)
        def _(p):
            at = pl.ds(pl.multiple_of(p * 256, 256), 256)
            two = [
                jnp.concatenate([wt[tile(2 * p + s), chip_rows(rel)] for rel in rels], axis=0)
                for s in (0, 1)
            ]
            got = jnp.dot(lhs, jnp.concatenate(two, axis=1), preferred_element_type=f32)
            if first:
                logits[:, at] = got
            else:
                logits[:, at] += got

    def hb_copy(k, size, peer, at_v):
        at = pl.ds(pl.multiple_of(at_v * dcol, 128), dcol)
        return pltpu.make_async_remote_copy(
            src_ref=hx.at[both(k, size)], dst_ref=hall.at[(*both(k, size), at)],
            send_sem=hb_s.at[k, peer], recv_sem=hb_r.at[k, at_v],
            device_id=(dp, peer), device_id_type=MESH,
        )

    def spread():
        for k in others:
            by_rows(k, lambda size: hx_copy(k, size, k).wait_recv())

            @pl.loop(1, nv)
            def _(j):
                peer = lax.rem(v + j, nv)
                by_rows(k, lambda size: hb_copy(k, size, peer, v).start())

            hall[pl.ds(2 * k, 2), :, mine] = hx[pl.ds(2 * k, 2)]

    def spread_done():
        for k in others:

            @pl.loop(1, nv)
            def _(j):
                peer = lax.rem(v + j, nv)
                by_rows(k, lambda size: hb_copy(k, size, peer, peer).wait_recv())

    near = min(arc - 1, far)
    begin = min(begin_at, arc)
    done = max(e for e in range(near + 1) if e == 0 or any(
        s >= begin and e < s and e in (2 * (s - begin) + 1, 2 * (s - begin) + 2)
        for s in range(1, arc + 1)))
    rest = tuple(range(done + 1, nz - done))
    top_size = -(-nt // nz)
    low = -(-top_size // 2)
    high = max(low, min(
        (-(-nt * (b + arc - 1) // nz) - -(-nt * b // nz)) // 2 for b in range(nz)))

    @pl.loop(1, arc + 1)
    def _(s):
        relay(s)
        pl.when(s == min(spread_at, arc - 1))(spread)

        @pl.when(s == begin)
        def _():
            spread_done()
            ready(0, 0, arc)
            accumulate((0,), True)

        for extra in range(2):
            e = 2 * (s - begin) + 1 + extra

            @pl.when((s >= begin) & (e <= near) & (e < s))
            def _():
                ready(nz - e, 0, arc)
                ready(e, 0, arc)
                accumulate((nz - e, e), False)

        @pl.when(s == max(arc - 1, begin))
        def _():
            if low < high:
                for rel in rest:
                    ready(rel, 1, arc - 1)
                accumulate(rest, False, low, high)

    for rel in rest:
        if low < high:
            ready(rel, 0, 1)
            ready(rel, arc - 1, arc)
        else:
            ready(rel, 0, arc)
    accumulate(rest, False, 0, low)
    accumulate(rest, False, high, pairs)

    for k in others:
        tg_copy(k, k).wait_recv()
    tl = []
    for k in range(groups):
        wide = jnp.broadcast_to(tg[k, 0:1, :], (128, 256))
        tl.append(jnp.transpose(wide)[0:seg, 0:1])
    local_t = jnp.concatenate(tl, axis=0) - (v * cols).astype(f32)

    def cut(p):
        return pl.ds(pl.multiple_of(p * 256, 256), 256)

    def ids(p):
        lane = lax.broadcasted_iota(jnp.int32, (1, 256), 1)
        low = lane < 128
        at = jnp.where(low, shard_tile(2 * p) * 128 + lane, shard_tile(2 * p + 1) * 128 + lane - 128)
        return at.astype(f32), lane + p * 256 < n_mine * 128

    def highest(p, top):
        ok = ids(p)[1]
        return jnp.maximum(top, jnp.max(jnp.where(ok, logits[:, cut(p)], -jnp.inf), axis=1, keepdims=True))

    peak = lax.fori_loop(0, pairs, highest, jnp.full((rows_n, 1), -jnp.inf, f32))

    def tally(p, carry):
        total, target = carry
        at, ok = ids(p)
        part = logits[:, cut(p)]
        total = total + jnp.sum(jnp.where(ok, jnp.exp(part - peak), 0.0), axis=1, keepdims=True)
        hit = (local_t == at) & ok
        target = target + jnp.sum(jnp.where(hit, part, 0.0), axis=1, keepdims=True)
        return total, target

    zero = jnp.zeros((rows_n, 1), f32)
    total, target = lax.fori_loop(0, pairs, tally, (zero, zero))
    lane = lax.broadcasted_iota(jnp.int32, (rows_n, 128), 1)
    table = jnp.where(lane == 0, peak, jnp.where(lane == 1, total, jnp.where(lane == 2, target, 0.0)))
    if lanes > rows_n:
        table = jnp.concatenate([table, jnp.zeros((lanes - rows_n, 128), f32)], axis=0)
    zstat[kz] = jnp.transpose(table)[0:8, :]

    def zst_copy(slot, to):
        return pltpu.make_async_remote_copy(
            src_ref=zstat.at[slot], dst_ref=zstat.at[slot],
            send_sem=zst_s.at[to], recv_sem=zst_r.at[slot],
            device_id=(plane_dev(to), v), device_id_type=MESH,
        )

    for to in others:
        zst_copy(kz, to).start()

    @pl.loop(1, far + 1)
    def _(e):
        for d in (0, 1):
            direct(d, e, sent)

    @pl.loop(0, arc - 1)
    def _(p):
        @pl.loop(1, far + p + 2)
        def _(e):
            for d in (0, 1):
                onward(d, p, e, sent)

    @pl.loop(0, arc)
    def _(x):
        @pl.loop(0, nz)
        def _(rel):
            by_tiles(base + x, lambda src, size: sib(rel, x, src, size, core).wait_send())

    for to in others:
        by_rows(kz, lambda size: hx_copy(kz, size, to).wait_send())
        tg_copy(kz, to).wait_send()

    @pl.loop(1, nv)
    def _(j):
        peer = lax.rem(v + j, nv)
        for k in others:
            by_rows(k, lambda size: hb_copy(k, size, peer, v).wait_send())

    for k in others:
        zst_copy(k, k).wait_recv()

    def joined(ref, n):
        top = ref[0, 0:1, :]
        for k in range(1, n):
            top = jnp.maximum(top, ref[k, 0:1, :])
        whole, hit = jnp.zeros_like(top), jnp.zeros_like(top)
        for k in range(n):
            whole = whole + ref[k, 1:2, :] * jnp.exp(ref[k, 0:1, :] - top)
            hit = hit + ref[k, 2:3, :]
        return top, whole, hit

    top, whole, hit = joined(zstat, groups)
    r8 = lax.broadcasted_iota(jnp.int32, (8, lanes), 0)
    stat[v] = jnp.where(r8 == 0, top, jnp.where(r8 == 1, whole, jnp.where(r8 == 2, hit, 0.0)))

    def stat_copy(peer, slot):
        return pltpu.make_async_remote_copy(
            src_ref=stat.at[slot], dst_ref=stat.at[slot],
            send_sem=stat_s.at[peer], recv_sem=stat_r.at[slot],
            device_id=(dp, peer), device_id_type=MESH,
        )

    @pl.loop(1, nv)
    def _(k):
        stat_copy(lax.rem(v + k, nv), v).start()

    @pl.loop(1, nv)
    def _(k):
        peer = lax.rem(v + k, nv)
        stat_copy(peer, peer).wait_recv()

    top, whole, hit = joined(stat, nv)
    log_total = top + jnp.log(whole)
    token = hit - log_total
    lt_col = jnp.transpose(jnp.broadcast_to(log_total, (128, lanes)))[0:rows_n, 0:1]

    @pl.loop(0, pairs)
    def _(p):
        at, ok = ids(p)
        soft = jnp.exp(logits[:, cut(p)] - lt_col)
        onehot = (local_t == at).astype(f32)
        gl[:, cut(p)] = jnp.where(ok, onehot - soft, 0.0).astype(bf16)

    def g_copy(k, size, peer, slot):
        return pltpu.make_async_remote_copy(
            src_ref=gsend.at[(peer, *both(k, size))], dst_ref=grecv.at[(slot, *both(k, size))],
            send_sem=g_s.at[k, peer], recv_sem=g_r.at[k, slot],
            device_id=(dp, peer), device_id_type=MESH,
        )

    npair = nv // 2

    @pl.loop(0, npair)
    def _(i):
        q = lax.rem(lax.div(v, 2) + i + 1, npair)
        at = pl.ds(pl.multiple_of(q * 2 * dcol, 128), 2 * dcol)
        got = jnp.zeros((rows_n, 2 * dcol), f32)
        for p in range(pairs):
            rhs = jnp.concatenate([wt[tile(2 * p), at], wt[tile(2 * p + 1), at]], axis=1)
            got = got + lax.dot_general(
                gl[:, p * 256 : (p + 1) * 256], rhs, (((1,), (1,)), ((), ())),
                preferred_element_type=f32,
            )
        got = got.astype(bf16).reshape(2 * groups, window, 2 * dcol)
        for side in (0, 1):
            peer = 2 * q + side
            gsend[peer] = got[:, :, side * dcol : (side + 1) * dcol]

            @pl.when(peer != v)
            def _():
                for k in others:
                    by_rows(k, lambda size: g_copy(k, size, peer, v).start())

    @pl.loop(2, nv + 2)
    def _(i):
        peer = lax.rem(2 * lax.div(v, 2) + i, nv)

        @pl.when(peer != v)
        def _():
            by_rows(kz, lambda size: g_copy(kz, size, peer, v).start())

    spot = lax.broadcasted_iota(jnp.int32, (1, lanes), 1) - kz * seg
    sums = []
    for m in (0, 1):
        inside = (spot >= m * window) & (spot < m * window + lens[m])
        sums.append(jnp.sum(jnp.where(inside, token, 0.0), axis=1, keepdims=True))
    refs = [refs_ref[0:1, m : m + 1] for m in (0, 1)]
    count = (lens[0] + lens[1]).astype(f32)
    ml = lax.broadcasted_iota(jnp.int32, (8, 128), 1)
    mr = lax.broadcasted_iota(jnp.int32, (8, 128), 0)
    word = jnp.zeros((8, 128), f32)
    for at, value in enumerate((sums[0], sums[1], refs[0], refs[1], count)):
        word = jnp.where((ml == at) & (mr == 0), value, word)
    msg[dp] = word

    def msg_copy(peer, slot):
        return pltpu.make_async_remote_copy(
            src_ref=msg.at[slot], dst_ref=msg.at[slot],
            send_sem=msg_s.at[peer], recv_sem=msg_r.at[slot],
            device_id=(peer, v), device_id_type=MESH,
        )

    @pl.loop(1, dp_n)
    def _(k):
        msg_copy(lax.rem(dp + k, dp_n), dp).start()

    def summed(k):
        @pl.loop(1, nv)
        def _(j):
            peer = lax.rem(v + j, nv)
            by_rows(k, lambda size: g_copy(k, size, peer, peer).wait_recv())

        return lax.fori_loop(
            1, nv,
            lambda j, acc: acc + grecv[lax.rem(v + j, nv), pl.ds(2 * k, 2)].astype(f32),
            gsend[v, pl.ds(2 * k, 2)].astype(f32),
        )

    def f_copy(k, size, slot, to):
        return pltpu.make_async_remote_copy(
            src_ref=fsend.at[both(k, size)], dst_ref=frecv.at[both(slot, size)],
            send_sem=f_s.at[k], recv_sem=f_r.at[slot],
            device_id=(plane_dev(to), v), device_id_type=MESH,
        )

    for k in others:
        fsend[pl.ds(2 * k, 2)] = summed(k).astype(bf16)
        by_rows(k, lambda size: f_copy(k, size, kz, k).start())

    @pl.loop(1, dp_n)
    def _(k):
        peer = lax.rem(dp + k, dp_n)
        msg_copy(peer, peer).wait_recv()

    board = jnp.sum(msg[...], axis=1)
    mean_length = jnp.sum(board[:, 4:5], axis=0, keepdims=True) / float(2 * dp_n)
    who = lax.broadcasted_iota(jnp.int32, (dp_n, 1), 0)
    weights = []
    loss_lane = lax.broadcasted_iota(jnp.int32, (1, 2), 1)
    losses = jnp.zeros((1, 2), f32)
    for m in (0, 1):
        gaps = board[:, m : m + 1] / mean_length - board[:, 2 + m : 3 + m]
        own_gap = sums[m] / mean_length - refs[m]
        partner = partner_ref[0:1, m : m + 1]
        partner_gap = jnp.sum(jnp.where(who == partner, gaps, 0.0), axis=0, keepdims=True)
        sign = jnp.where(dp < partner, 1.0, -1.0)
        margin = margin_beta * sign * (own_gap - partner_gap)
        small = jnp.exp(-jnp.abs(margin))
        loss = jnp.maximum(-margin, 0.0) + jnp.log1p(small)
        sig = jnp.where(margin >= 0, small, 1.0) / (1.0 + small)
        weights.append(-loss_scale * margin_beta * sign * sig / mean_length)
        losses = jnp.where(loss_lane == m, loss, losses)
    loss_ref[...] = losses

    grads = summed(kz)

    for to in others:
        by_rows(to, lambda size: f_copy(to, size, kz, to).wait_send())
        zst_copy(kz, to).wait_send()

    @pl.loop(1, nv)
    def _(j):
        peer = lax.rem(v + j, nv)
        stat_copy(peer, v).wait_send()
        for k in [kz] + others:
            by_rows(k, lambda size: g_copy(k, size, peer, v).wait_send())

    @pl.loop(1, dp_n)
    def _(k):
        msg_copy(lax.rem(dp + k, dp_n), dp).wait_send()

    for k in others:
        by_rows(kz, lambda size: f_copy(k, size, k, k).wait_recv())
        grads = grads + frecv[pl.ds(2 * k, 2)].astype(f32)
    for m in (0, 1):
        part = jnp.where(masks[m], grads[m] * weights[m], 0.0)
        pos = lax.broadcasted_iota(jnp.int32, (128, window), 0)
        row = lax.broadcasted_iota(jnp.int32, (128, window), 1)
        back = (pos == row + starts[m]).astype(f32)
        grad_ref[m] = jnp.dot(
            back, part, preferred_element_type=f32, precision=lax.Precision.HIGHEST
        )


def solution(mesh):
    dp_n, nv = mesh.shape["dp"], mesh.shape["vocab"]
    nz = dp_n // 2
    arc = nz // groups
    far = (nz - arc) // 2

    def body(hidden, out_weight, targets, prompt_start, response_len, partner, ref_scores):
        micro, seqs, length, depth = hidden.shape
        kr, cols = out_weight.shape
        nt = cols // 128
        most = max(-(-nt * (z + arc) // nz) - -(-nt * z // nz) for z in range(nz))
        wide = -(-most // 2) * 256
        seg = 2 * window
        rows_n = groups * seg
        lanes = -(-rows_n // 128) * 128
        dcol = depth // nv
        f32, bf16, i32 = jnp.float32, jnp.bfloat16, jnp.int32
        vm = pl.BlockSpec(memory_space=pltpu.VMEM)
        hbm = pl.BlockSpec(memory_space=pltpu.HBM)
        dma = pltpu.SemaphoreType.DMA
        mem = pltpu.VMEM
        loss, grad = pl.pallas_call(
            functools.partial(kernel, dp_n, nv),
            out_shape=(
                jax.ShapeDtypeStruct((1, micro), f32),
                jax.ShapeDtypeStruct((micro, length, dcol), f32),
            ),
            in_specs=[hbm] * 7,
            out_specs=(vm, vm),
            scratch_shapes=[
                mem((micro * length, depth), bf16),
                mem((micro, length), i32),
                mem((1, micro), i32), mem((1, micro), i32), mem((1, micro), i32),
                mem((1, micro), f32),
                mem((nt, depth, 128), bf16),
                mem((2 * groups, window, depth), bf16),
                mem((2 * groups, window, dcol), bf16),
                mem((groups, 8, 256), f32),
                mem((rows_n, wide), f32),
                mem((rows_n, wide), bf16),
                mem((nv, 8, lanes), f32),
                mem((groups, 8, lanes), f32),
                mem((nv, 2 * groups, window, dcol), bf16),
                mem((nv, 2 * groups, window, dcol), bf16),
                mem((2 * groups, window, dcol), bf16),
                mem((2 * groups, window, dcol), bf16),
                mem((dp_n, 8, 128), f32),
                dma((6,)), dma((nt,)),
                dma((2, arc, far + arc)), dma((2, arc, far + arc)),
                dma((nz, arc)), dma((nz, arc)),
                dma((groups,)), dma((groups,)),
                dma((groups,)), dma((groups,)),
                dma((groups, nv)), dma((groups, nv)),
                dma((groups,)), dma((groups,)),
                dma((nv,)), dma((nv,)),
                dma((dp_n,)), dma((dp_n,)),
                dma((groups, nv)), dma((groups, nv)),
                dma((groups,)), dma((groups,)),
            ],
            compiler_params=pltpu.CompilerParams(
                collective_id=0, has_side_effects=True, vmem_limit_bytes=56 * 1024 * 1024
            ),
        )(
            hidden.reshape(micro * length, depth),
            out_weight,
            targets.reshape(micro, length),
            prompt_start.reshape(1, micro),
            response_len.reshape(1, micro),
            partner.reshape(1, micro),
            ref_scores.reshape(1, micro),
        )
        return loss.reshape(micro, seqs), grad.reshape(micro, seqs, length, dcol)

    return jax.shard_map(
        body,
        mesh=mesh,
        in_specs=(
            P(None, "dp", None, None),
            P("dp", "vocab"),
            P(None, "dp", None),
            P(None, "dp"),
            P(None, "dp"),
            P(None, "dp"),
            P(None, "dp"),
        ),
        out_specs=(P(None, "dp"), P(None, "dp", None, "vocab")),
        check_vma=False,
    )
```

time: 120 us -> 114 us (0.950)
  local copies, waits for them, and re-layouts: 6.77 us -> 2.72 us
  Pallas kernels: 112 us -> 110 us
    unnamed x20 -> x4, local copies, waits for them, and re-layouts: 6.77 us -> 2.72 us
    pallas_call x1, Pallas kernels: 112 us -> 110 us  [body(): pl.pallas_call(functools.partial(kernel, dp_n, nv), out_shape=(jax.ShapeD...]
where the time goes in v2:
time: 114 us
  Pallas kernels  110 us (96%)
  local copies, waits for them, and re-layouts  2.72 us (2%)
    pallas_call x1, Pallas kernels, body(): pl.pallas_call(functools.partial(kernel, dp_n, nv), out_shape=(jax.ShapeD...  110 us
    unnamed x4, local copies, waits for them, and re-layouts  2.72 us

profile of v2, /device:TPU:1, one launch (start us, length us, event | category | flops | bytes accessed | tf_op | source)
XLA Modules:
  0.0 113.8 jit_solution(4767969954302158768)
XLA Ops:
  0.6 110.4 %shard_map.86 = (f32[1,2]{1,0:T(1,128)}, f32[2,128,128]{2,1,0:T(8,128)}) custom-call(bf16[256,2048]{1,0:T(8,128)(2,1)} %bitcast.10, bf16[64,3200]{1,0:T(8,128)(2,1)} %w_hbm.1, s32[2,128]{1,0:T(2,128)} %bitcast.12, s32[1,2]{1,0:T(1,128)} %bitcast.13, s32[1,2]{1,0:T(1,128)} %bitcast.14, s32[1,2]{1,0:T(1,128)} %bitcast.15, f32[1,2]{1,0:T(1,128)} %bitcast.16), custom_call_target="tpu_custom_call" | custom-call | tf_op jit(solution)/shard_map/pallas_call | solution.py:635
  111.1 0.0 copy-start
  111.1 0.6 copy-done
  111.7 0.5 copy.12
  112.2 1.6 %copy.13 = f32[2,1,128,128]{3,2,1,0:T(8,128)} copy(f32[2,1,128,128]{3,2,1,0:T(8,128)} %bitcast.11) | data formatting | bytes 262144
Async XLA Ops:
  111.1 0.7 copy-start

commit v3 on v2

--- a/solution.py
+++ b/solution.py
@@ -21,8 +21,9 @@
     loss_ref, grad_ref,
     h_ref, t_ref, start_ref, len_ref, partner_ref, refs_ref,
     wt, hall, hx, tg, logits, gl, stat, zstat, gsend, grecv, fsend, frecv, msg,
+    oh, osend, orecv, osum, oback, columns,
     in_sem, own_sem, ring_s, ring_r, sib_s, sib_r, hx_s, hx_r, tg_s, tg_r, hb_s, hb_r,
-    zst_s, zst_r, stat_s, stat_r, msg_s, msg_r, g_s, g_r, f_s, f_r,
+    zst_s, zst_r, stat_s, stat_r, msg_s, msg_r, g_s, g_r, f_s, f_r, o_s, o_r, fo_s, fo_r,
 ):
     f32, bf16 = jnp.float32, jnp.bfloat16
     dp, v = lax.axis_index("dp"), lax.axis_index("vocab")
@@ -300,6 +301,59 @@
                 peer = lax.rem(v + j, nv)
                 by_rows(k, lambda size: hb_copy(k, size, peer, peer).wait_recv())
 
+    def local_targets():
+        tl = []
+        for k in range(groups):
+            wide = jnp.broadcast_to(tg[k, 0:1, :], (128, 256))
+            tl.append(jnp.transpose(wide)[0:seg, 0:1])
+        return jnp.concatenate(tl, axis=0) - (v * cols).astype(f32)
+
+    def cut(p):
+        return pl.ds(pl.multiple_of(p * 256, 256), 256)
+
+    def ids(p):
+        lane = lax.broadcasted_iota(jnp.int32, (1, 256), 1)
+        low = lane < 128
+        at = jnp.where(low, shard_tile(2 * p) * 128 + lane, shard_tile(2 * p + 1) * 128 + lane - 128)
+        return at.astype(f32), lane + p * 256 < n_mine * 128
+
+    def find_targets():
+        for k in others:
+            tg_copy(k, k).wait_recv()
+        local = local_targets()
+
+        @pl.loop(0, pairs)
+        def _(p):
+            at, ok = ids(p)
+            oh[:, cut(p)] = ((local == at) & ok).astype(f32).astype(bf16)
+
+    def o_copy(k, size, peer, slot):
+        return pltpu.make_async_remote_copy(
+            src_ref=osend.at[(peer, *both(k, size))], dst_ref=orecv.at[(slot, *both(k, size))],
+            send_sem=o_s.at[k, peer], recv_sem=o_r.at[k, slot],
+            device_id=(dp, peer), device_id_type=MESH,
+        )
+
+    npair = nv // 2
+
+    def blocks(lhs, out, send):
+        @pl.loop(0, npair)
+        def _(i):
+            q = lax.rem(lax.div(v, 2) + i + 1, npair)
+            at = pl.ds(pl.multiple_of(q * 2 * dcol, 128), 2 * dcol)
+            got = jnp.zeros((rows_n, 2 * dcol), f32)
+            for p in range(pairs):
+                rhs = jnp.concatenate([wt[tile(2 * p), at], wt[tile(2 * p + 1), at]], axis=1)
+                got = got + lax.dot_general(
+                    lhs[:, p * 256 : (p + 1) * 256], rhs, (((1,), (1,)), ((), ())),
+                    preferred_element_type=f32,
+                )
+            got = got.astype(bf16).reshape(2 * groups, window, 2 * dcol)
+            for side in (0, 1):
+                peer = 2 * q + side
+                out[peer] = got[:, :, side * dcol : (side + 1) * dcol]
+                pl.when(peer != v)(functools.partial(send, peer))
+
     near = min(arc - 1, far)
     begin = min(begin_at, arc)
     done = max(e for e in range(near + 1) if e == 0 or any(
@@ -321,6 +375,7 @@
             spread_done()
             ready(0, 0, arc)
             accumulate((0,), True)
+            find_targets()
 
         for extra in range(2):
             e = 2 * (s - begin) + 1 + extra
@@ -347,22 +402,7 @@
     accumulate(rest, False, 0, low)
     accumulate(rest, False, high, pairs)
 
-    for k in others:
-        tg_copy(k, k).wait_recv()
-    tl = []
-    for k in range(groups):
-        wide = jnp.broadcast_to(tg[k, 0:1, :], (128, 256))
-        tl.append(jnp.transpose(wide)[0:seg, 0:1])
-    local_t = jnp.concatenate(tl, axis=0) - (v * cols).astype(f32)
-
-    def cut(p):
-        return pl.ds(pl.multiple_of(p * 256, 256), 256)
-
-    def ids(p):
-        lane = lax.broadcasted_iota(jnp.int32, (1, 256), 1)
-        low = lane < 128
-        at = jnp.where(low, shard_tile(2 * p) * 128 + lane, shard_tile(2 * p + 1) * 128 + lane - 128)
-        return at.astype(f32), lane + p * 256 < n_mine * 128
+    local_t = local_targets()
 
     def highest(p, top):
         ok = ids(p)[1]
@@ -374,8 +414,9 @@
         total, target = carry
         at, ok = ids(p)
         part = logits[:, cut(p)]
-        total = total + jnp.sum(jnp.where(ok, jnp.exp(part - peak), 0.0), axis=1, keepdims=True)
         hit = (local_t == at) & ok
+        rest_of = jnp.where(ok & (local_t != at), jnp.exp(part - peak), 0.0)
+        total = total + jnp.sum(rest_of, axis=1, keepdims=True)
         target = target + jnp.sum(jnp.where(hit, part, 0.0), axis=1, keepdims=True)
         return total, target
 
@@ -385,17 +426,24 @@
     table = jnp.where(lane == 0, peak, jnp.where(lane == 1, total, jnp.where(lane == 2, target, 0.0)))
     if lanes > rows_n:
         table = jnp.concatenate([table, jnp.zeros((lanes - rows_n, 128), f32)], axis=0)
-    zstat[kz] = jnp.transpose(table)[0:8, :]
-
-    def zst_copy(slot, to):
-        return pltpu.make_async_remote_copy(
-            src_ref=zstat.at[slot], dst_ref=zstat.at[slot],
-            send_sem=zst_s.at[to], recv_sem=zst_r.at[slot],
-            device_id=(plane_dev(to), v), device_id_type=MESH,
-        )
-
-    for to in others:
-        zst_copy(kz, to).start()
+    stat[v] = jnp.transpose(table)[0:8, :]
+
+    def stat_copy(peer, slot):
+        return pltpu.make_async_remote_copy(
+            src_ref=stat.at[slot], dst_ref=stat.at[slot],
+            send_sem=stat_s.at[peer], recv_sem=stat_r.at[slot],
+            device_id=(dp, peer), device_id_type=MESH,
+        )
+
+    @pl.loop(1, nv)
+    def _(k):
+        stat_copy(lax.rem(v + k, nv), v).start()
+
+    def send_targets(peer):
+        for k in others + [kz]:
+            by_rows(k, lambda size: o_copy(k, size, peer, v).start())
+
+    blocks(oh, osend, send_targets)
 
     @pl.loop(1, far + 1)
     def _(e):
@@ -425,8 +473,10 @@
         for k in others:
             by_rows(k, lambda size: hb_copy(k, size, peer, v).wait_send())
 
-    for k in others:
-        zst_copy(k, k).wait_recv()
+    @pl.loop(1, nv)
+    def _(k):
+        peer = lax.rem(v + k, nv)
+        stat_copy(peer, peer).wait_recv()
 
     def joined(ref, n):
         top = ref[0, 0:1, :]
@@ -438,37 +488,26 @@
             hit = hit + ref[k, 2:3, :]
         return top, whole, hit
 
-    top, whole, hit = joined(zstat, groups)
+    top, whole, hit = joined(stat, nv)
     r8 = lax.broadcasted_iota(jnp.int32, (8, lanes), 0)
-    stat[v] = jnp.where(r8 == 0, top, jnp.where(r8 == 1, whole, jnp.where(r8 == 2, hit, 0.0)))
-
-    def stat_copy(peer, slot):
-        return pltpu.make_async_remote_copy(
-            src_ref=stat.at[slot], dst_ref=stat.at[slot],
-            send_sem=stat_s.at[peer], recv_sem=stat_r.at[slot],
-            device_id=(dp, peer), device_id_type=MESH,
-        )
-
-    @pl.loop(1, nv)
-    def _(k):
-        stat_copy(lax.rem(v + k, nv), v).start()
-
-    @pl.loop(1, nv)
-    def _(k):
-        peer = lax.rem(v + k, nv)
-        stat_copy(peer, peer).wait_recv()
-
-    top, whole, hit = joined(stat, nv)
-    log_total = top + jnp.log(whole)
-    token = hit - log_total
-    lt_col = jnp.transpose(jnp.broadcast_to(log_total, (128, lanes)))[0:rows_n, 0:1]
+    zstat[kz] = jnp.where(r8 == 0, top, jnp.where(r8 == 1, whole, jnp.where(r8 == 2, hit, 0.0)))
+
+    def zst_copy(slot, to):
+        return pltpu.make_async_remote_copy(
+            src_ref=zstat.at[slot], dst_ref=zstat.at[slot],
+            send_sem=zst_s.at[to], recv_sem=zst_r.at[slot],
+            device_id=(plane_dev(to), v), device_id_type=MESH,
+        )
+
+    for to in others:
+        zst_copy(kz, to).start()
+    top_col = jnp.transpose(jnp.broadcast_to(top, (128, lanes)))[0:rows_n, 0:1]
 
     @pl.loop(0, pairs)
     def _(p):
         at, ok = ids(p)
-        soft = jnp.exp(logits[:, cut(p)] - lt_col)
-        onehot = (local_t == at).astype(f32)
-        gl[:, cut(p)] = jnp.where(ok, onehot - soft, 0.0).astype(bf16)
+        soft = jnp.exp(logits[:, cut(p)] - top_col)
+        gl[:, cut(p)] = jnp.where(ok & (local_t != at), soft, 0.0).astype(bf16)
 
     def g_copy(k, size, peer, slot):
         return pltpu.make_async_remote_copy(
@@ -477,28 +516,11 @@
             device_id=(dp, peer), device_id_type=MESH,
         )
 
-    npair = nv // 2
-
-    @pl.loop(0, npair)
-    def _(i):
-        q = lax.rem(lax.div(v, 2) + i + 1, npair)
-        at = pl.ds(pl.multiple_of(q * 2 * dcol, 128), 2 * dcol)
-        got = jnp.zeros((rows_n, 2 * dcol), f32)
-        for p in range(pairs):
-            rhs = jnp.concatenate([wt[tile(2 * p), at], wt[tile(2 * p + 1), at]], axis=1)
-            got = got + lax.dot_general(
-                gl[:, p * 256 : (p + 1) * 256], rhs, (((1,), (1,)), ((), ())),
-                preferred_element_type=f32,
-            )
-        got = got.astype(bf16).reshape(2 * groups, window, 2 * dcol)
-        for side in (0, 1):
-            peer = 2 * q + side
-            gsend[peer] = got[:, :, side * dcol : (side + 1) * dcol]
-
-            @pl.when(peer != v)
-            def _():
-                for k in others:
-                    by_rows(k, lambda size: g_copy(k, size, peer, v).start())
+    def send_partner(peer):
+        for k in others:
+            by_rows(k, lambda size: g_copy(k, size, peer, v).start())
+
+    blocks(gl, gsend, send_partner)
 
     @pl.loop(2, nv + 2)
     def _(i):
@@ -507,6 +529,17 @@
         @pl.when(peer != v)
         def _():
             by_rows(kz, lambda size: g_copy(kz, size, peer, v).start())
+
+    for k in others:
+        zst_copy(k, k).wait_recv()
+    top, whole, hit = joined(zstat, groups)
+    every = whole + jnp.exp(hit - top)
+    token = hit - top - jnp.log(every)
+    r128 = lax.broadcasted_iota(jnp.int32, (128, lanes), 0)
+    factors = jnp.where(r128 == 0, whole / every, 0.0)
+    for at, k in enumerate([kz] + others):
+        factors = jnp.where(r128 == 1 + at, jnp.exp(zstat[k, 0:1, :] - top) / every, factors)
+    columns[...] = jnp.transpose(factors)
 
     spot = lax.broadcasted_iota(jnp.int32, (1, lanes), 1) - kz * seg
     sums = []
@@ -533,16 +566,23 @@
     def _(k):
         msg_copy(lax.rem(dp + k, dp_n), dp).start()
 
-    def summed(k):
+    def summed(k, copy, out, into):
         @pl.loop(1, nv)
         def _(j):
             peer = lax.rem(v + j, nv)
-            by_rows(k, lambda size: g_copy(k, size, peer, peer).wait_recv())
+            by_rows(k, lambda size: copy(k, size, peer, peer).wait_recv())
 
         return lax.fori_loop(
             1, nv,
-            lambda j, acc: acc + grecv[lax.rem(v + j, nv), pl.ds(2 * k, 2)].astype(f32),
-            gsend[v, pl.ds(2 * k, 2)].astype(f32),
+            lambda j, acc: acc + into[lax.rem(v + j, nv), pl.ds(2 * k, 2)].astype(f32),
+            out[v, pl.ds(2 * k, 2)].astype(f32),
+        )
+
+    def fo_copy(k, size, slot, to):
+        return pltpu.make_async_remote_copy(
+            src_ref=osum.at[both(k, size)], dst_ref=oback.at[both(slot, size)],
+            send_sem=fo_s.at[k], recv_sem=fo_r.at[slot],
+            device_id=(plane_dev(to), v), device_id_type=MESH,
         )
 
     def f_copy(k, size, slot, to):
@@ -553,7 +593,9 @@
         )
 
     for k in others:
-        fsend[pl.ds(2 * k, 2)] = summed(k).astype(bf16)
+        osum[pl.ds(2 * k, 2)] = summed(k, o_copy, osend, orecv).astype(bf16)
+        by_rows(k, lambda size: fo_copy(k, size, kz, k).start())
+        fsend[pl.ds(2 * k, 2)] = summed(k, g_copy, gsend, grecv).astype(bf16)
         by_rows(k, lambda size: f_copy(k, size, kz, k).start())
 
     @pl.loop(1, dp_n)
@@ -581,10 +623,12 @@
         losses = jnp.where(loss_lane == m, loss, losses)
     loss_ref[...] = losses
 
-    grads = summed(kz)
+    found = summed(kz, o_copy, osend, orecv)
+    grads = summed(kz, g_copy, gsend, grecv)
 
     for to in others:
         by_rows(to, lambda size: f_copy(to, size, kz, to).wait_send())
+        by_rows(to, lambda size: fo_copy(to, size, kz, to).wait_send())
         zst_copy(kz, to).wait_send()
 
     @pl.loop(1, nv)
@@ -593,14 +637,20 @@
         stat_copy(peer, v).wait_send()
         for k in [kz] + others:
             by_rows(k, lambda size: g_copy(k, size, peer, v).wait_send())
+            by_rows(k, lambda size: o_copy(k, size, peer, v).wait_send())
 
     @pl.loop(1, dp_n)
     def _(k):
         msg_copy(lax.rem(dp + k, dp_n), dp).wait_send()
 
-    for k in others:
+    scale = columns[seg_rows(kz), :].reshape(2, window, 128)
+    grads = grads * scale[:, :, 1:2]
+    for at, k in enumerate(others):
+        by_rows(kz, lambda size: fo_copy(k, size, k, k).wait_recv())
+        found = found + oback[pl.ds(2 * k, 2)].astype(f32)
         by_rows(kz, lambda size: f_copy(k, size, k, k).wait_recv())
-        grads = grads + frecv[pl.ds(2 * k, 2)].astype(f32)
+        grads = grads + frecv[pl.ds(2 * k, 2)].astype(f32) * scale[:, :, 2 + at : 3 + at]
+    grads = found * scale[:, :, 0:1] - grads
     for m in (0, 1):
         part = jnp.where(masks[m], grads[m] * weights[m], 0.0)
         pos = lax.broadcasted_iota(jnp.int32, (128, window), 0)
@@ -658,6 +708,12 @@
                 mem((2 * groups, window, dcol), bf16),
                 mem((2 * groups, window, dcol), bf16),
                 mem((dp_n, 8, 128), f32),
+                mem((rows_n, wide), bf16),
+                mem((nv, 2 * groups, window, dcol), bf16),
+                mem((nv, 2 * groups, window, dcol), bf16),
+                mem((2 * groups, window, dcol), bf16),
+                mem((2 * groups, window, dcol), bf16),
+                mem((lanes, 128), f32),
                 dma((6,)), dma((nt,)),
                 dma((2, arc, far + arc)), dma((2, arc, far + arc)),
                 dma((nz, arc)), dma((nz, arc)),
@@ -667,6 +723,8 @@
                 dma((groups,)), dma((groups,)),
                 dma((nv,)), dma((nv,)),
                 dma((dp_n,)), dma((dp_n,)),
+                dma((groups, nv)), dma((groups, nv)),
+                dma((groups,)), dma((groups,)),
                 dma((groups, nv)), dma((groups, nv)),
                 dma((groups,)), dma((groups,)),
             ],

time: 114 us -> 114 us (level)
  no operation moved by 1% of the time
where the time goes in v3:
time: 114 us; the launch traced here: 113 us
  Pallas kernels  110 us (96%)
  local copies, waits for them, and re-layouts  2.72 us (2%)
    pallas_call x1, Pallas kernels, body(): pl.pallas_call(functools.partial(kernel, dp_n, nv), out_shape=(jax.ShapeD...  110 us
    unnamed x4, local copies, waits for them, and re-layouts  2.72 us

profile of v3, /device:TPU:1, one launch (start us, length us, event | category | flops | bytes accessed | tf_op | source)
XLA Modules:
  0.0 113.3 jit_solution(298653050457037474)
XLA Ops:
  0.6 109.9 %shard_map.86 = (f32[1,2]{1,0:T(1,128)}, f32[2,128,128]{2,1,0:T(8,128)}) custom-call(bf16[256,2048]{1,0:T(8,128)(2,1)} %bitcast.10, bf16[64,3200]{1,0:T(8,128)(2,1)} %w_hbm.1, s32[2,128]{1,0:T(2,128)} %bitcast.12, s32[1,2]{1,0:T(1,128)} %bitcast.13, s32[1,2]{1,0:T(1,128)} %bitcast.14, s32[1,2]{1,0:T(1,128)} %bitcast.15, f32[1,2]{1,0:T(1,128)} %bitcast.16), custom_call_target="tpu_custom_call" | custom-call | tf_op jit(solution)/shard_map/pallas_call | solution.py:685
  110.6 0.0 copy-start
  110.6 0.6 copy-done
  111.2 0.5 copy.12
  111.7 1.6 %copy.13 = f32[2,1,128,128]{3,2,1,0:T(8,128)} copy(f32[2,1,128,128]{3,2,1,0:T(8,128)} %bitcast.11) | data formatting | bytes 262144
Async XLA Ops:
  110.6 0.7 copy-start
